TPU v7x, 32 devices: a whole 2x2x4 slice. The times are simulated.
32 devices in a mesh: lvl: 2 (over core), front: 4 (over z), grid: 4 (over y, x).
Axes of the slice: x: 2, y: 2, z: 4, core: 2. Of those that a mesh axis runs over, the one named last changes fastest.
Arguments:
- child_panel: bfloat16 [4, 2, 4, 2, 128, 512], P('front', None, 'grid', 'lvl'), may hold values from -0.6 to 0.6
- child_blocks: int32 [4], P('front'), may hold values from 6 to 8, as said below
- tile_rows: int32 [2, 4, 4, 64], P('lvl', 'front', 'grid'), may hold values from 0 to 1
- tile_cols: int32 [2, 4, 4, 64], P('lvl', 'front', 'grid'), may hold values from 0 to 7
- tile_parent: int32 [2, 4, 4, 64, 1], P('lvl', 'front', 'grid'), may hold values from 0 to 3; in each aligned block of 64 rows (0 to 63, 64 to 127, ..., all dimensions but the last counted through in order) at most 32 rows name the same one
- tile_place: int32 [2, 4, 4, 64], P('lvl', 'front', 'grid'), may hold values from 0 to 15
- parent_owner: int32 [4], replicated, may hold values from 0 to 3, each once
- parent_front: float32 [4, 2, 4, 2, 128, 2048], P('front', None, 'grid', 'lvl'), may hold values from -1.5 to 151.5, as said below
Outputs:
- factored: float32 [4, 2, 4, 2, 128, 2048], P('front', None, 'grid', 'lvl')
Inputs may be any that keep to these rules, and one draw needn't show every extreme that they name: `child_blocks`: some child front has exactly 8 blocks. `tile_parent`: among the 64 tiles of one device at most 32 name the same parent front, and some parent front is named by exactly 32. `parent_owner`: each front index holds exactly one parent. `parent_front`: the diagonal of each parent's first diagonal block lies between 148.5 and 151.5; all other entries lie within -1.5 to 1.5.
All inputs are finite; a program needn't handle non-finite values.
Results may differ from a plain program's by a relative error of at most 0.00053.
Values may be sent and summed in bfloat16 or wider, within the bound.
A program may use at most 64 MiB of HBM per device.

v0:
```python
import jax
import jax.numpy as jnp
from jax import lax
from jax.sharding import PartitionSpec as P

BLOCK = 256


def broadcast(block, axis, source):
    block = jnp.where(lax.axis_index(axis) == source, block, jnp.zeros_like(block))
    return lax.psum(block, axis)


def per_device(
    child_panel,
    child_blocks,
    tile_rows,
    tile_cols,
    tile_parent,
    tile_place,
    parent_owner,
    parent_front,
):
    level_count = lax.axis_size("lvl")
    grid_count = lax.axis_size("grid")
    front_count = lax.axis_size("front")
    grid_index = lax.axis_index("grid")
    child_local = child_panel.shape[1]
    half_rows = child_panel.shape[4]
    panel_width = child_panel.shape[5]
    parent_local = parent_front.shape[1]
    front_width = parent_front.shape[5]
    block_count = front_width // BLOCK
    slot_count = tile_rows.shape[3]
    capacity = 2 * slot_count // front_count
    slot_total = front_count * capacity
    own_rows = child_panel.reshape(child_local, half_rows, panel_width)
    gathered = lax.all_gather(
        own_rows.reshape(1, child_local, half_rows, panel_width),
        ("lvl", "grid"),
        axis=0,
        tiled=True,
    )
    panel_view = gathered.reshape(level_count, grid_count, child_local, half_rows, panel_width)
    row_local = tile_rows.reshape(slot_count)
    col_block = tile_cols.reshape(slot_count)
    col_grid = col_block % grid_count
    col_local = col_block // grid_count

    def tile_group(indices):

        def one_tile(row_pick, grid_pick, local_pick):
            left_rows = own_rows[row_pick]
            right_rows = panel_view[:, grid_pick, local_pick].reshape(BLOCK, panel_width)
            product = jnp.einsum(
                "ik,jk->ij", left_rows, right_rows, preferred_element_type=jnp.float32
            )
            return (-product).astype(jnp.bfloat16)

        return jax.vmap(one_tile)(indices[0], indices[1], indices[2])

    grouped = (
        jnp.stack([row_local, col_grid, col_local])
        .reshape(3, 8, slot_count // 8)
        .transpose(1, 0, 2)
    )
    update_tiles = lax.map(tile_group, grouped).reshape(slot_count, half_rows, BLOCK)
    child_size = child_blocks[0]
    live_tile = (row_local * grid_count + grid_index < child_size) & (col_block < child_size)
    update_tiles = jnp.where(live_tile[:, None, None], update_tiles, jnp.zeros((), jnp.bfloat16))
    parents = tile_parent.reshape(slot_count)
    places = tile_place.reshape(slot_count)
    front_ids = jnp.arange(front_count, dtype=jnp.int32)
    owners = jnp.sum(
        jnp.where(parents[:, None] == front_ids[None, :], parent_owner[None, :], 0), axis=1
    )
    one_hot = (owners[:, None] == front_ids[None, :]).astype(jnp.int32)
    rank_within = jnp.sum((jnp.cumsum(one_hot, axis=0) - 1) * one_hot, axis=1)
    slot_index = owners * capacity + rank_within
    matches = slot_index[None, :] == jnp.arange(slot_total, dtype=jnp.int32)[:, None]
    filled = jnp.any(matches, axis=1)
    source = jnp.sum(
        jnp.where(matches, jnp.arange(slot_count, dtype=jnp.int32)[None, :], 0), axis=1
    )
    outgoing = jnp.where(filled[:, None, None], update_tiles[source], jnp.zeros((), jnp.bfloat16))
    positions = jnp.where(filled, places[source], -1)
    incoming, landed = (
        lax.all_to_all(outgoing, "front", split_axis=0, concat_axis=0, tiled=True),
        lax.all_to_all(positions, "front", split_axis=0, concat_axis=0, tiled=True),
    )
    spots = parent_local * block_count
    selector = (landed[:, None] == jnp.arange(spots, dtype=jnp.int32)[None, :]).astype(jnp.bfloat16)
    contrib = jnp.einsum("sk,sij->kij", selector, incoming, preferred_element_type=jnp.float32)
    contrib = (
        contrib.reshape(parent_local, block_count, half_rows, BLOCK)
        .transpose(0, 2, 1, 3)
        .reshape(parent_local, half_rows, front_width)
    )
    assembled = parent_front.reshape(parent_local, half_rows, front_width) + contrib
    own_half = assembled[0, :, :BLOCK]
    joined = lax.all_gather(own_half, "lvl", axis=0, tiled=True)
    pivot_block = broadcast(joined, "grid", 0)
    pivot_block = 0.5 * (pivot_block + pivot_block.T)
    lower_factor = jnp.linalg.cholesky(pivot_block)
    first_column = assembled[:, :, :BLOCK].reshape(parent_local * half_rows, BLOCK)
    panel_rows = lax.linalg.triangular_solve(
        lower_factor, first_column, left_side=False, lower=True, transpose_a=True
    )
    panel_rows = panel_rows.reshape(parent_local, half_rows, BLOCK)
    shared = lax.all_gather(
        panel_rows.reshape(1, parent_local, half_rows, BLOCK), ("lvl", "grid"), axis=0, tiled=True
    )
    shared = shared.reshape(level_count, grid_count, parent_local, half_rows, BLOCK)
    schur = jnp.einsum("rik,lgsjk->risglj", panel_rows, shared, precision=lax.Precision.HIGHEST)
    schur = schur.reshape(parent_local, half_rows, front_width)
    trailing = assembled[:, :, BLOCK:] - schur[:, :, BLOCK:]
    result = jnp.concatenate([panel_rows, trailing], axis=2)
    return result.reshape(1, parent_local, 1, 1, half_rows, front_width)


def solution(mesh):
    return jax.shard_map(
        per_device,
        mesh=mesh,
        in_specs=(
            P("front", None, "grid", "lvl", None, None),
            P("front"),
            P("lvl", "front", "grid", None),
            P("lvl", "front", "grid", None),
            P("lvl", "front", "grid", None, None),
            P("lvl", "front", "grid", None),
            P(),
            P("front", None, "grid", "lvl", None, None),
        ),
        out_specs=P("front", None, "grid", "lvl", None, None),
        check_vma=False,
    )
```

profile of v0, /device:TPU:0, one launch (start us, length us, event | category | flops | bytes accessed | tf_op | source)
XLA Modules:
  0.0 450.2 jit_solution(15282769628164825725)
XLA Ops:
  7.3 0.8 select_reduce_fusion.4
  8.6 1.2 gather_fusion.2
  10.6 6.3 %all-to-all-start = ((s32[4,32,1]{1,2,0:T(1,128)}), s32[4,32,1]{1,2,0:T(1,128)S(1)}, u32[]{:S(2)}, u32[]{:S(2)}) async-start(s32[4,32,1]{1,2,0:T(1,128)} %bitcast.12), calls=%async_computation | async-start | bytes 4096 | tf_op jit(solution)/shard_map/all_to_all | solution.py:89
  17.5 1.3 reduce.21
  18.8 1.3 reduce.22
  21.6 18.3 %all-gather.7.cloned.1.call-done = bf16[8,2,1,1,128,512]{5,4,3,2,1,0:T(8,128)(2,1)} async-done(((bf16[1,2,1,1,128,512]{5,4,3,2,1,0:T(8,128)(2,1)}), bf16[8,2,1,1,128,512]{5,4,3,2,1,0:T(8,128)(2,1)}) %all-gather.7.cloned.1.call-update) | async-done | bytes 2097168 | tf_op jit(solution)/shard_map/all_gather | solution.py:38
  39.9 3.1 copy.49
  43.0 36.4 %while.11 = (s32[]{:T(128)}, bf16[8,8,128,256]{3,2,1,0:T(8,128)(2,1)}, s32[8,3,8]{2,0,1:T(8,128)S(1)}, bf16[2,128,512]{2,1,0:T(8,128)(2,1)S(1)}, bf16[2,4,2,128,...) while((s32[]{:T(128)}, bf16[8,8,128,256]{3,2,1,0:T(8,128)(2,1)}, s32[8,3,8]{2,0,1:T(8,128)S(1)}, ...), condition=%wide.region_6.7_spmd, body=%wide.region_5.6_spmd.sunk | while | flops 268959872 | bytes 9962529 | solution.py:67
  43.1 2.3 gather_fusion.1
  46.0 1.6 fusion.43
  47.6 2.3 gather_fusion.1
  50.5 1.6 fusion.43
  52.1 2.3 gather_fusion.1
  55.1 1.6 fusion.43
  56.7 2.3 gather_fusion.1
  59.6 1.6 fusion.43
  61.3 2.3 gather_fusion.1
  64.2 1.6 fusion.43
  65.8 2.3 gather_fusion.1
  68.7 1.6 fusion.43
  70.4 2.3 gather_fusion.1
  73.3 1.6 fusion.43
  74.9 2.3 gather_fusion.1
  77.8 1.6 fusion.43
  79.4 4.5 bitcast_select_fusion
  83.9 8.7 %gather_fusion.3 = bf16[128,128,256]{2,1,0:T(8,128)(2,1)} fusion(bf16[64,128,256]{2,1,0:T(8,128)(2,1)} %bitcast_select_fusion, s32[1024]{0:T(1024)S(1)} %pad_clamp_fusion), kind=kCustom, calls=%fused_computation.3 | custom fusion | bytes 16777728 | tf_op jit(solution)/shard_map/gather | solution.py:85
  92.6 7.2 %broadcast_select_fusion = bf16[128,128,256]{2,1,0:T(8,128)(2,1)} fusion(bf16[128,128,256]{2,1,0:T(8,128)(2,1)} %gather_fusion.3, pred[128]{0:T(512)(128)(4,1)S(1)} %fusion.20), kind=kLoop, calls=%fused_computation.23 | loop fusion | flops 4194304 | bytes 16777344 | tf_op jit(solution)/shard_map/jit(_where)/select_n | solution.py:85
  99.8 5.8 %all-to-all-start.1 = ((bf16[128,128,256]{2,1,0:T(8,128)(2,1)}), bf16[128,128,256]{2,1,0:T(8,128)(2,1)}, u32[]{:S(2)}, u32[]{:S(2)}) async-start(bf16[128,128,256]{2,1,0:T(8,128)(2,1)} %broadcast_select_fusion), calls=%async_computation.1 | async-start | bytes 16777216 | tf_op jit(solution)/shard_map/all_to_all | solution.py:88
  105.7 1.9 copy.46
  108.3 181.1 %all-to-all-done.1 = bf16[128,128,256]{2,1,0:T(8,128)(2,1)} async-done(((bf16[128,128,256]{2,1,0:T(8,128)(2,1)}), bf16[128,128,256]{2,1,0:T(8,128)(2,1)}, u32[]{:S(2)}, u32[]{:S(2)}) %all-to-all-start.1) | async-done | bytes 8388640 | tf_op jit(solution)/shard_map/all_to_all | solution.py:88
  289.4 7.9 %fusion.8 = f32[2,8,128,256]{3,1,0,2:T(8,128)S(1)} fusion(bf16[128,128,256]{2,1,0:T(8,128)(2,1)} %all-to-all-done.1, s32[128]{0:T(128)S(1)} %eq.71), kind=kOutput, calls=%fused_computation.28 | convolution fusion | flops 134219776 | bytes 10486272 | tf_op jit(solution)/shard_map/sk,sij->kij/dot_general | solution.py:93
  297.3 1.9 copy.51
  299.2 2.4 bitcast_add_fusion
  301.6 2.0 all-gather.1
  304.8 40.8 %all-reduce.4.cloned.1.call-done = f32[256,256]{0,1:T(8,128)} async-done(((f32[256,256]{0,1:T(8,128)}), f32[256,256]{0,1:T(8,128)}) %all-reduce.4.cloned.1.call-update) | async-done | bytes 262160 | tf_op jit(solution)/shard_map/psum | solution.py:11
  345.6 1.1 copy.53
  346.7 1.0 fusion.12
  347.9 11.7 %cholesky.49 = f32[128,128]{1,0:T(8,128)S(1)} custom-call(f32[128,128]{1,0:T(8,128)S(1)} %cholesky.115), custom_call_target="Cholesky" | custom-call | tf_op jit(solution)/shard_map/jit(cholesky)/cholesky | solution.py:104
  359.7 9.8 %custom-call.14 = f32[1,128,128]{1,2,0:T(8,128)S(1)} custom-call(f32[1,128,128]{2,1,0:T(8,128)S(1)} %get-tuple-element.86), custom_call_target="InvertDiagBlocksLowerTriangular" | custom-call | tf_op jit(solution)/shard_map/jit(cholesky)/cholesky | solution.py:104
  370.0 11.7 %cholesky.103 = f32[128,128]{1,0:T(8,128)S(1)} custom-call(f32[128,128]{1,0:T(8,128)S(1)} %convolution_subtract_fusion.1), custom_call_target="Cholesky" | custom-call | tf_op jit(solution)/shard_map/jit(cholesky)/cholesky | solution.py:104
  383.9 4.3 while.12
  384.7 1.4 bitcast_dynamic-update-slice_fusion.2
  386.7 1.4 bitcast_dynamic-update-slice_fusion.2
  388.2 19.7 %custom-call.15 = f32[2,128,128]{1,2,0:T(8,128)S(1)} custom-call(f32[2,128,128]{2,1,0:T(8,128)S(1)} %get-tuple-element.40), custom_call_target="InvertDiagBlocksLowerTriangular" | custom-call | tf_op jit(solution)/shard_map/triangular_solve | solution.py:106
  409.8 1.1 copy.58
  410.9 27.0 %all-gather.5.cloned.1.call-done = f32[8,2,128,256]{3,2,1,0:T(8,128)} async-done(((f32[1,2,128,256]{3,2,1,0:T(8,128)}), f32[8,2,128,256]{3,2,1,0:T(8,128)}) %all-gather.5.cloned.1.call-update) | async-done | bytes 2097168 | tf_op jit(solution)/shard_map/all_gather | solution.py:110
  437.8 3.4 convolution_bitcast_fusion
  441.8 1.8 copy.59
  (79 shorter events, 15.5 us)
Async XLA Ops:
  6.5 2.1 copy-start
  6.5 33.4 %all-gather.7.cloned.1.call-start = ((), (), s32[]{:S(2)}) async-start(), calls=%async_computation.4 | async-start | bytes 2359296 | tf_op jit(solution)/shard_map/all_gather | solution.py:38
  10.6 89.2 %all-to-all-start = ((s32[4,32,1]{1,2,0:T(1,128)}), s32[4,32,1]{1,2,0:T(1,128)S(1)}, u32[]{:S(2)}, u32[]{:S(2)}) async-start(s32[4,32,1]{1,2,0:T(1,128)} %bitcast.12), calls=%async_computation | async-start | bytes 4096 | tf_op jit(solution)/shard_map/all_to_all | solution.py:89
  39.9 3.1 copy-start.2
  99.8 5.9 %copy-start.3 = (f32[1,2,1,1,128,2048]{5,4,3,2,1,0:T(8,128)S(1)}, f32[1,2,1,1,128,2048]{5,4,3,2,1,0:T(8,128)}, u32[]{:S(2)}) copy-start(f32[1,2,1,1,128,2048]{5,4,3,2,1,0:T(8,128)} %param.17) | copy-start | bytes 6291460
  99.8 189.6 %all-to-all-start.1 = ((bf16[128,128,256]{2,1,0:T(8,128)(2,1)}), bf16[128,128,256]{2,1,0:T(8,128)(2,1)}, u32[]{:S(2)}, u32[]{:S(2)}) async-start(bf16[128,128,256]{2,1,0:T(8,128)(2,1)} %broadcast_select_fusion), calls=%async_computation.1 | async-start | bytes 16777216 | tf_op jit(solution)/shard_map/all_to_all | solution.py:88
  105.6 240.0 %all-reduce.4.cloned.1.call-start = ((), (), s32[]{:S(2)}) async-start(), calls=%async_computation.2 | async-start | bytes 524288 | tf_op jit(solution)/shard_map/psum | solution.py:11
  304.4 133.4 %all-gather.5.cloned.1.call-start = ((), (), s32[]{:S(2)}) async-start(), calls=%async_computation.3 | async-start | bytes 2359296 | tf_op jit(solution)/shard_map/all_gather | solution.py:110
  441.7 2.0 copy-start.1
Sparse Core Ops, SparseCore 0:
  9.2 30.6 all-gather.6
  304.5 41.0 all-reduce.3
  409.9 27.8 all-gather.4
where the time goes:
time: 451 us; the launch traced here: 450 us
  waiting for transfers between devices  268 us (59%)
  other arithmetic  75.5 us (17%)
  local copies, waits for them, and re-layouts  50.8 us (11%)
  matrix products  25.8 us (6%)
  between operations  15.4 us (3%)
  starting transfers between devices  12.4 us (3%)
    all_to_all x1, waiting for transfers between devices, per_device(): lax.all_to_all(outgoing, 'front', split_axis=0, concat_axis=0, tiled=True)  181 us
    psum x1, waiting for transfers between devices, broadcast(): return lax.psum(block, axis)  40.8 us
    another operation x6, other arithmetic, per_device(): lower_factor = jnp.linalg.cholesky(pivot_block)  34 us
    all_gather x1, waiting for transfers between devices, per_device(): lax.all_gather(panel_rows.reshape(1, parent_local, half_rows, BLOCK), ('l...  27 us
    another operation x4, other arithmetic, per_device(): lax.linalg.triangular_solve(lower_factor, first_column, left_side=False,...  19.7 us
    all_gather x1, waiting for transfers between devices, per_device(): lax.all_gather(own_rows.reshape(1, child_local, half_rows, panel_width),...  18.3 us
    gather x8, local copies, waits for them, and re-layouts, one_tile(): panel_view[:, grid_pick, local_pick].reshape(BLOCK, panel_width)  18.2 us
    dot_general x8, matrix products, one_tile(): jnp.einsum('ik,jk->ij', left_rows, right_rows, preferred_element_type=jnp...  13 us
  transfers between devices with their start and end apart: 5, of which 4 were waited for; matrix products, arithmetic and copies ran while one was open for 16% of the time, Pallas kernels for 0%

commit v1 on v0

--- a/solution.py
+++ b/solution.py
@@ -8,7 +8,7 @@
 
 def broadcast(block, axis, source):
     block = jnp.where(lax.axis_index(axis) == source, block, jnp.zeros_like(block))
-    return lax.psum(block, axis)
+    return jnp.sum(lax.all_gather(block, axis), axis=0)
 
 
 def per_device(

time: 451 us -> 441 us (0.978)
  waiting for transfers between devices: 268 us -> 254 us
    psum x1 -> x0, waiting for transfers between devices: 40.8 us -> none  [broadcast(): return lax.psum(block, axis)]
    all_gather x0 -> x1, waiting for transfers between devices: none -> 24.6 us  [broadcast(): return jnp.sum(lax.all_gather(block, axis), axis=0)]
  transfers between devices with their start and end apart: 5 -> 5, of which waited for: 4 -> 4; matrix products, arithmetic and copies ran while one was open for 16% -> 15% of each run, Pallas kernels for 0% -> 0%
where the time goes in v1:
time: 441 us; the launch traced here: 440 us
  waiting for transfers between devices  254 us (58%)
  other arithmetic  79.9 us (18%)
  local copies, waits for them, and re-layouts  49.7 us (11%)
  matrix products  25.8 us (6%)
  between operations  15.4 us (3%)
  starting transfers between devices  12.2 us (3%)
    all_to_all x1, waiting for transfers between devices, per_device(): lax.all_to_all(outgoing, 'front', split_axis=0, concat_axis=0, tiled=True)  183 us
    another operation x6, other arithmetic, per_device(): lower_factor = jnp.linalg.cholesky(pivot_block)  34 us
    all_gather x1, waiting for transfers between devices, per_device(): lax.all_gather(panel_rows.reshape(1, parent_local, half_rows, BLOCK), ('l...  27.7 us
    all_gather x1, waiting for transfers between devices, broadcast(): return jnp.sum(lax.all_gather(block, axis), axis=0)  24.6 us
    another operation x4, other arithmetic, per_device(): lax.linalg.triangular_solve(lower_factor, first_column, left_side=False,...  19.7 us
    all_gather x1, waiting for transfers between devices, per_device(): lax.all_gather(own_rows.reshape(1, child_local, half_rows, panel_width),...  18.3 us
    gather x8, local copies, waits for them, and re-layouts, one_tile(): panel_view[:, grid_pick, local_pick].reshape(BLOCK, panel_width)  18.2 us
    dot_general x8, matrix products, one_tile(): jnp.einsum('ik,jk->ij', left_rows, right_rows, preferred_element_type=jnp...  13 us
  transfers between devices with their start and end apart: 5, of which 4 were waited for; matrix products, arithmetic and copies ran while one was open for 15% of the time, Pallas kernels for 0%

profile of v1, /device:TPU:0, one launch (start us, length us, event | category | flops | bytes accessed | tf_op | source)
XLA Modules:
  0.0 439.8 jit_solution(12493500229311847285)
XLA Ops:
  7.3 0.8 select_reduce_fusion.4
  8.6 1.2 gather_fusion.2
  10.6 6.3 %all-to-all-start = ((s32[4,32,1]{1,2,0:T(1,128)}), s32[4,32,1]{1,2,0:T(1,128)S(1)}, u32[]{:S(2)}, u32[]{:S(2)}) async-start(s32[4,32,1]{1,2,0:T(1,128)} %bitcast.12), calls=%async_computation | async-start | bytes 4096 | tf_op jit(solution)/shard_map/all_to_all | solution.py:89
  17.5 1.3 reduce.21
  18.9 1.3 reduce.22
  21.6 18.3 %all-gather.10.cloned.1.call-done = bf16[8,2,1,1,128,512]{5,4,3,2,1,0:T(8,128)(2,1)} async-done(((bf16[1,2,1,1,128,512]{5,4,3,2,1,0:T(8,128)(2,1)}), bf16[8,2,1,1,128,512]{5,4,3,2,1,0:T(8,128)(2,1)}) %all-gather.10.cloned.1.call-update) | async-done | bytes 2097168 | tf_op jit(solution)/shard_map/all_gather | solution.py:38
  39.9 3.1 copy.53
  43.0 36.4 %while.11 = (s32[]{:T(128)}, bf16[8,8,128,256]{3,2,1,0:T(8,128)(2,1)}, s32[8,3,8]{2,0,1:T(8,128)S(1)}, bf16[2,128,512]{2,1,0:T(8,128)(2,1)S(1)}, bf16[2,4,2,128,...) while((s32[]{:T(128)}, bf16[8,8,128,256]{3,2,1,0:T(8,128)(2,1)}, s32[8,3,8]{2,0,1:T(8,128)S(1)}, ...), condition=%wide.region_6.7_spmd, body=%wide.region_5.6_spmd.sunk | while | flops 268959872 | bytes 9962529 | solution.py:67
  43.0 2.3 gather_fusion.1
  45.9 1.6 fusion.43
  47.6 2.3 gather_fusion.1
  50.5 1.6 fusion.43
  52.1 2.3 gather_fusion.1
  55.0 1.6 fusion.43
  56.7 2.3 gather_fusion.1
  59.6 1.6 fusion.43
  61.2 2.3 gather_fusion.1
  64.1 1.6 fusion.43
  65.8 2.3 gather_fusion.1
  68.7 1.6 fusion.43
  70.3 2.3 gather_fusion.1
  73.3 1.6 fusion.43
  74.9 2.3 gather_fusion.1
  77.8 1.6 fusion.43
  79.4 4.5 %bitcast_select_fusion = bf16[64,128,256]{2,1,0:T(8,128)(2,1)} fusion(bf16[8,8,128,256]{3,2,1,0:T(8,128)(2,1)} %get-tuple-element.32, pred[64]{0:T(512)(128)(4,1)S(1)} %and_bitcast_fusion), kind=kLoop, calls=%fused_computation.24 | loop fusion | flops 2097152 | bytes 8388672 | tf_op jit(solution)/shard_map/jit(_where)/select_n | solution.py:70
  83.9 8.7 %gather_fusion.3 = bf16[128,128,256]{2,1,0:T(8,128)(2,1)} fusion(bf16[64,128,256]{2,1,0:T(8,128)(2,1)} %bitcast_select_fusion, s32[1024]{0:T(1024)S(1)} %pad_clamp_fusion), kind=kCustom, calls=%fused_computation.3 | custom fusion | bytes 16777728 | tf_op jit(solution)/shard_map/gather | solution.py:85
  92.6 7.2 %broadcast_select_fusion = bf16[128,128,256]{2,1,0:T(8,128)(2,1)} fusion(bf16[128,128,256]{2,1,0:T(8,128)(2,1)} %gather_fusion.3, pred[128]{0:T(512)(128)(4,1)S(1)} %fusion.21), kind=kLoop, calls=%fused_computation.23 | loop fusion | flops 4194304 | bytes 16777344 | tf_op jit(solution)/shard_map/jit(_where)/select_n | solution.py:85
  99.8 5.7 %all-to-all-start.1 = ((bf16[128,128,256]{2,1,0:T(8,128)(2,1)}), bf16[128,128,256]{2,1,0:T(8,128)(2,1)}, u32[]{:S(2)}, u32[]{:S(2)}) async-start(bf16[128,128,256]{2,1,0:T(8,128)(2,1)} %broadcast_select_fusion), calls=%async_computation.1 | async-start | bytes 16777216 | tf_op jit(solution)/shard_map/all_to_all | solution.py:88
  106.2 183.0 %all-to-all-done.1 = bf16[128,128,256]{2,1,0:T(8,128)(2,1)} async-done(((bf16[128,128,256]{2,1,0:T(8,128)(2,1)}), bf16[128,128,256]{2,1,0:T(8,128)(2,1)}, u32[]{:S(2)}, u32[]{:S(2)}) %all-to-all-start.1) | async-done | bytes 8388640 | tf_op jit(solution)/shard_map/all_to_all | solution.py:88
  289.3 7.9 %fusion.8 = f32[2,128,8,256]{3,2,0,1:T(8,128)S(1)} fusion(bf16[128,128,256]{2,1,0:T(8,128)(2,1)} %all-to-all-done.1, s32[128]{0:T(128)S(1)} %eq.71), kind=kOutput, calls=%fused_computation.28 | convolution fusion | flops 134219776 | bytes 10486272 | tf_op jit(solution)/shard_map/sk,sij->kij/dot_general | solution.py:93
  297.2 2.3 reshape.400
  299.5 3.5 copy_add_fusion
  303.0 2.0 all-gather.1
  306.0 24.6 %all-gather.12.cloned.1.call-done = f32[1,1024,256]{2,1,0:T(8,128)} async-done(((f32[1,256,256]{2,1,0:T(8,128)}), f32[1,1024,256]{2,1,0:T(8,128)}) %all-gather.12.cloned.1.call-update) | async-done | bytes 1048592 | tf_op jit(solution)/shard_map/all_gather | solution.py:11
  330.7 1.3 reduce_sum.42
  332.2 11.7 %cholesky.49 = f32[128,128]{1,0:T(8,128)S(1)} custom-call(f32[128,128]{1,0:T(8,128)S(1)} %cholesky.115), custom_call_target="Cholesky" | custom-call | tf_op jit(solution)/shard_map/jit(cholesky)/cholesky | solution.py:104
  344.0 9.8 %custom-call.14 = f32[1,128,128]{1,2,0:T(8,128)S(1)} custom-call(f32[1,128,128]{2,1,0:T(8,128)S(1)} %get-tuple-element.91), custom_call_target="InvertDiagBlocksLowerTriangular" | custom-call | tf_op jit(solution)/shard_map/jit(cholesky)/cholesky | solution.py:104
  354.3 11.7 %cholesky.103 = f32[128,128]{1,0:T(8,128)S(1)} custom-call(f32[128,128]{1,0:T(8,128)S(1)} %convolution_subtract_fusion.1), custom_call_target="Cholesky" | custom-call | tf_op jit(solution)/shard_map/jit(cholesky)/cholesky | solution.py:104
  368.2 4.3 while.12
  369.0 1.4 bitcast_dynamic-update-slice_fusion.2
  371.0 1.4 bitcast_dynamic-update-slice_fusion.2
  372.5 19.7 %custom-call.15 = f32[2,128,128]{1,2,0:T(8,128)S(1)} custom-call(f32[2,128,128]{2,1,0:T(8,128)S(1)} %get-tuple-element.40), custom_call_target="InvertDiagBlocksLowerTriangular" | custom-call | tf_op jit(solution)/shard_map/triangular_solve | solution.py:106
  394.4 27.7 %all-gather.8.cloned.1.call-done = f32[8,2,128,256]{3,2,1,0:T(8,128)} async-done(((f32[1,2,128,256]{3,2,1,0:T(8,128)}), f32[8,2,128,256]{3,2,1,0:T(8,128)}) %all-gather.8.cloned.1.call-update) | async-done | bytes 2097168 | tf_op jit(solution)/shard_map/all_gather | solution.py:110
  422.1 3.4 convolution_bitcast_fusion
  425.7 1.4 slice.98
  427.1 2.8 copy.70
  429.9 1.8 slice_subtract_fusion
  431.7 1.6 maximum_bitcast_fusion
  (76 shorter events, 15.3 us)
Async XLA Ops:
  6.5 2.1 copy-start
  6.5 33.3 %all-gather.10.cloned.1.call-start = ((), (), s32[]{:S(2)}) async-start(), calls=%async_computation.3 | async-start | bytes 2359296 | tf_op jit(solution)/shard_map/all_gather | solution.py:38
  10.6 89.2 %all-to-all-start = ((s32[4,32,1]{1,2,0:T(1,128)}), s32[4,32,1]{1,2,0:T(1,128)S(1)}, u32[]{:S(2)}, u32[]{:S(2)}) async-start(s32[4,32,1]{1,2,0:T(1,128)} %bitcast.12), calls=%async_computation | async-start | bytes 4096 | tf_op jit(solution)/shard_map/all_to_all | solution.py:89
  39.9 3.1 copy-start.2
  99.8 189.5 %all-to-all-start.1 = ((bf16[128,128,256]{2,1,0:T(8,128)(2,1)}), bf16[128,128,256]{2,1,0:T(8,128)(2,1)}, u32[]{:S(2)}, u32[]{:S(2)}) async-start(bf16[128,128,256]{2,1,0:T(8,128)(2,1)} %broadcast_select_fusion), calls=%async_computation.1 | async-start | bytes 16777216 | tf_op jit(solution)/shard_map/all_to_all | solution.py:88
  105.5 225.2 %all-gather.12.cloned.1.call-start = ((), (), s32[]{:S(2)}) async-start(), calls=%async_computation.4 | async-start | bytes 1310720 | tf_op jit(solution)/shard_map/all_gather | solution.py:11
  305.7 116.4 %all-gather.8.cloned.1.call-start = ((), (), s32[]{:S(2)}) async-start(), calls=%async_computation.2 | async-start | bytes 2359296 | tf_op jit(solution)/shard_map/all_gather | solution.py:110
  429.8 3.4 copy-start.1
Sparse Core Ops, SparseCore 0:
  9.2 30.5 all-gather.9
  305.9 24.7 all-gather.11
  394.2 27.8 all-gather.7
